TPU v7x, 128 devices: a whole 4x4x4 slice. The times are simulated.
128 devices in a mesh: wide: 32 (over y_lo, x, z), narrow: 4 (over y_hi, core).
Axes of the slice: x: 4, y: 4 (y_hi: 2, y_lo: 2; y = y_hi * 2 + y_lo), z: 4, core: 2. Of those that a mesh axis runs over, the one named last changes fastest.
Arguments:
- trial_x: float32 [262144, 128], P(('wide', 'narrow')), may hold values from -6 to 6
- trial_y: float32 [262144, 128], P(('wide', 'narrow')), may hold values from -6 to 6
- energy: float32 [262144], P(('wide', 'narrow')), may hold values from 1 to 4
- level_shift: float32 [128], replicated, may hold values from 0.1 to 0.5
- resonant_kernel: bfloat16 [1024, 8, 256, 256], P(('wide', 'narrow')), may hold values from -0.0625 to 0.0625
- resonant_list: int32 [1024, 8], P(('wide', 'narrow')), may hold values from 0 to 31, all different within a row
- coupling_kernel: bfloat16 [1024, 8, 256, 256], P(('wide', 'narrow')), may hold values from -0.0625 to 0.0625
- coupling_list: int32 [1024, 8], P(('wide', 'narrow')), may hold values from 0 to 31, all different within a row
- partner: int32 [32, 8192], P('wide'), may hold values from 0 to 8191, each once within a row
- exchange_basis: bfloat16 [262144, 1024], P(('wide', 'narrow')), may hold values from -0.0234375 to 0.0234375
Outputs:
- new_x: float32 [262144, 128], P(('wide', 'narrow'))
- new_y: float32 [262144, 128], P(('wide', 'narrow'))
Inputs may be any that keep to these rules, and one draw needn't show every extreme that they name: `resonant_list`: each row lists 8 different column blocks. `coupling_list`: each row lists 8 different column blocks. `partner`: each row is a permutation of the patch rows.
All inputs are finite; a program needn't handle non-finite values.
Results may differ from a plain program's by a relative error of at most 0.0038.
Values may be sent and summed in bfloat16 or wider, within the bound.
No kernel may reach another device: no remote copies, remote signals or barrier semaphores. Data moves between devices by JAX's collectives and lax.ppermute only.
A program may use at most 128 MiB of HBM per device.

v0:
```python
import jax
import jax.numpy as jnp
from jax import lax
from jax.sharding import PartitionSpec as P

BLK = 256
APPS = 2


def swapped(array, axis, stride):
    return lax.ppermute(array, axis, [(i, i ^ 1 << stride) for i in range(lax.axis_size(axis))])


def block_product(kernel, source, indices):
    columns = source.shape[1]
    tiles = source[indices]
    result = jnp.einsum("bnij,bnjc->bic", kernel, tiles, preferred_element_type=jnp.float32)
    return result.reshape(-1, columns)


def mirror_rows(stacked):
    top_bit = lax.axis_size("wide").bit_length() - 2
    moved = swapped(stacked, "wide", top_bit)
    return lax.all_gather(moved, "narrow", axis=0, tiled=True)


def exchange_term(summed, exchange_basis):
    partial_sum = lax.dot_general(
        exchange_basis, summed, (((0,), (0,)), ((), ())), preferred_element_type=jnp.float32
    )
    weights = lax.psum(partial_sum, ("wide", "narrow"))
    return jnp.dot(exchange_basis, weights.astype(jnp.bfloat16), preferred_element_type=jnp.float32)


def apply_once(
    trial_x,
    trial_y,
    energy,
    level_shift,
    resonant_kernel,
    resonant_list,
    coupling_kernel,
    coupling_list,
    partner,
    exchange_basis,
):
    vectors = trial_x.shape[1]
    stacked = jnp.concatenate([trial_x.astype(jnp.bfloat16), trial_y.astype(jnp.bfloat16)], axis=1)
    own_patch = lax.all_gather(stacked, "narrow", axis=0, tiled=True)
    mirror_patch = mirror_rows(stacked)
    offsets = jnp.arange(BLK, dtype=jnp.int32)
    own_indices = resonant_list[:, :, None] * BLK + offsets
    resonant = block_product(resonant_kernel, own_patch, own_indices)
    partner_indices = partner[0].reshape(-1, BLK)[coupling_list]
    coupling = block_product(coupling_kernel, mirror_patch, partner_indices)
    summed = (trial_x + trial_y).astype(jnp.bfloat16)
    exchange = exchange_term(summed, exchange_basis)
    levels = energy[:, None]
    shifts = level_shift[None, :]
    image_x = levels * trial_x + resonant[:, :vectors] + coupling[:, vectors:] + exchange
    image_y = -(levels * trial_y + resonant[:, vectors:] + coupling[:, :vectors] + exchange)
    next_x = (image_x - shifts * trial_x) / (levels - shifts)
    next_y = -(image_y - shifts * trial_y) / (levels + shifts)
    return (next_x, next_y)


def on_device(
    trial_x,
    trial_y,
    energy,
    level_shift,
    resonant_kernel,
    resonant_list,
    coupling_kernel,
    coupling_list,
    partner,
    exchange_basis,
):
    current_x, current_y = (trial_x, trial_y)
    for app_index in range(APPS):
        current_x, current_y = apply_once(
            current_x,
            current_y,
            energy,
            level_shift,
            resonant_kernel,
            resonant_list,
            coupling_kernel,
            coupling_list,
            partner,
            exchange_basis,
        )
    return (current_x, current_y)


def solution(mesh):
    return jax.shard_map(
        on_device,
        mesh=mesh,
        in_specs=(
            P(("wide", "narrow"), None),
            P(("wide", "narrow"), None),
            P(("wide", "narrow")),
            P(),
            P(("wide", "narrow"), None, None, None),
            P(("wide", "narrow"), None),
            P(("wide", "narrow"), None, None, None),
            P(("wide", "narrow"), None),
            P("wide", None),
            P(("wide", "narrow"), None),
        ),
        out_specs=(P(("wide", "narrow"), None), P(("wide", "narrow"), None)),
        check_vma=False,
    )
```

profile of v0, /device:TPU:1, one launch (start us, length us, event | category | flops | bytes accessed | tf_op | source)
XLA Modules:
  0.0 613.9 jit_solution(15115098581168945599)
XLA Ops:
  7.3 1.4 convert_element_type.24
  8.7 1.3 convert_element_type.25
  10.0 1.1 pad_maximum_fusion
  11.1 2.2 collective-permute-start
  13.3 32.0 %collective-permute-done = bf16[2048,256]{1,0:T(8,128)(2,1)S(1)} collective-permute-done((bf16[2048,256]{1,0:T(8,128)(2,1)}, bf16[2048,256]{1,0:T(8,128)(2,1)S(1)}, u32[]{:S(2)}, u32[]{:S(2)}) %collective-permute-start) | collective-permute-done | bytes 1048608 | tf_op jit(solution)/shard_map/ppermute | solution.py:11
  45.3 1.0 copy-done.3
  46.3 0.0 all-gather.9.cloned.1.call-start
  46.3 2.6 copy.12
  48.9 1.3 copy.16
  50.2 0.5 broadcast.86
  50.7 0.7 reduce.3
  51.5 0.1 reshape.62
  51.6 0.7 gather_fusion.1
  52.3 0.1 fusion.2
  52.4 2.9 convolution_bitcast_fusion.3
  55.4 96.2 %all-reduce.2 = bf16[1024,128]{0,1:T(8,128)(2,1)S(1)} all-reduce(f32[1024,128]{0,1:T(8,128)S(1)} %convolution_bitcast_fusion.3), channel_id=1, replica_groups=mesh['wide'=32,'narrow'=4] {'wide','narrow'}, use_global_device_ids=true, to_apply=%region_0.0 | all-reduce | flops 131072 | bytes 786432 | tf_op jit(solution)/shard_map/psum | solution.py:31
  151.6 63.6 %gather_fusion = bf16[16384,256]{1,0:T(8,128)(2,1)} fusion(bf16[8192,256]{1,0:T(8,128)(2,1)} %all-gather.5.cloned.1.call-done, s32[16384]{0:T(1024)S(1)} %broadcast_clamp_fusion.1), kind=kCustom, calls=%fused_computation | custom fusion | bytes 16842752 | tf_op jit(solution)/shard_map/gather | solution.py:16
  215.2 8.1 %fusion.10 = f32[8,256,256,1]{1,2,3,0:T(8,128)S(1)} fusion(bf16[8,8,256,256]{3,2,1,0:T(8,128)(2,1)} %param.14, bf16[8,8,256,256]{3,2,1,0:T(8,128)(2,1)} %bitcast.62), kind=kOutput, calls=%fused_computation.34 | convolution fusion | flops 2147483648 | bytes 18874368 | tf_op jit(solution)/shard_map/bnij,bnjc->bic/dot_general | solution.py:17
  223.3 0.1 fusion.8
  223.5 1.4 copy.32
  224.8 1.3 copy.34
  226.1 63.6 %gather_fusion.2 = bf16[16384,256]{1,0:T(8,128)(2,1)} fusion(bf16[8192,256]{1,0:T(8,128)(2,1)} %all-gather.7.cloned.1.call-done, s32[16384]{0:T(1024)S(1)} %broadcast_clamp_fusion), kind=kCustom, calls=%fused_computation.2 | custom fusion | bytes 16842752 | tf_op jit(solution)/shard_map/gather | solution.py:16
  289.8 8.1 %fusion.11 = f32[8,256,256,1]{1,2,3,0:T(8,128)S(1)} fusion(bf16[8,8,256,256]{3,2,1,0:T(8,128)(2,1)} %param.16, bf16[8,8,256,256]{3,2,1,0:T(8,128)(2,1)} %bitcast.63), kind=kOutput, calls=%fused_computation.35 | convolution fusion | flops 2147483648 | bytes 18874368 | tf_op jit(solution)/shard_map/bnij,bnjc->bic/dot_general | solution.py:17
  297.9 0.1 fusion.9
  298.0 1.3 copy.33
  299.4 0.3 copy.35
  299.7 6.6 %fusion.5 = (bf16[2048,128]{0,1:T(8,128)(2,1)S(1)}, f32[2048,128]{0,1:T(8,128)}, bf16[2048,128]{0,1:T(8,128)(2,1)S(1)}, f32[2048,128]{0,1:T(8,128)}) fusion(f32[2048,128]{0,1:T(8,128)} %copy.16, f32[128]{0:T(128)S(1)} %copy-done.9, f32[2048,128]{0,1:T(8,128)S(1)} %copy.35, f32[2048,128]{0,1:T(8,128)} %copy.34, f32[2048]{0:T(1024)S(1)} %copy-done.8, ...), kind=kOutput, calls=%fused_computation.29 | convolution fusion | flops 542113792 | bytes 13902336 | tf_op jit(solution)/shard_map/dot_general | solution.py:32
  306.4 1.0 pad_maximum_fusion.1
  307.5 0.3 collective-permute-start.1
  307.7 40.2 %collective-permute-done.1 = bf16[2048,256]{0,1:T(8,128)(2,1)S(1)} collective-permute-done((bf16[2048,256]{0,1:T(8,128)(2,1)}, bf16[2048,256]{0,1:T(8,128)(2,1)S(1)}, u32[]{:S(2)}, u32[]{:S(2)}) %collective-permute-start.1) | collective-permute-done | bytes 1048608 | tf_op jit(solution)/shard_map/ppermute | solution.py:11
  348.0 1.0 copy-done.4
  349.0 3.5 convolution_bitcast_fusion.2
  352.5 84.9 %all-reduce.3 = bf16[1024,128]{0,1:T(8,128)(2,1)S(1)} all-reduce(f32[1024,128]{0,1:T(8,128)S(1)} %convolution_bitcast_fusion.2), channel_id=1, replica_groups=mesh['wide'=32,'narrow'=4] {'wide','narrow'}, use_global_device_ids=true, to_apply=%region_1.0 | all-reduce | flops 131072 | bytes 786432 | tf_op jit(solution)/shard_map/psum | solution.py:31
  437.5 6.4 %copy.20 = bf16[8192,256]{1,0:T(8,128)(2,1)} copy(bf16[8192,256]{0,1:T(8,128)(2,1)} %all-gather.9.cloned.1.call-done) | data formatting | bytes 8388608 | tf_op jit(solution)/shard_map/all_gather | solution.py:49
  443.9 63.6 %gather_fusion.3 = bf16[16384,256]{1,0:T(8,128)(2,1)} fusion(bf16[8192,256]{1,0:T(8,128)(2,1)} %copy.20, s32[16384]{0:T(1024)S(1)} %broadcast_clamp_fusion.1), kind=kCustom, calls=%fused_computation.3 | custom fusion | bytes 16842752 | tf_op jit(solution)/shard_map/gather | solution.py:16
  507.5 8.1 %fusion.12 = f32[8,256,256,1]{1,2,3,0:T(8,128)S(1)} fusion(bf16[8,8,256,256]{3,2,1,0:T(8,128)(2,1)} %param.14, bf16[8,8,256,256]{3,2,1,0:T(8,128)(2,1)} %bitcast.60), kind=kOutput, calls=%fused_computation.36 | convolution fusion | flops 2147483648 | bytes 18874368 | tf_op jit(solution)/shard_map/bnij,bnjc->bic/dot_general | solution.py:17
  515.6 0.1 fusion.6
  515.7 0.3 copy.36
  516.1 1.3 copy.38
  517.4 6.4 %copy.22 = bf16[8192,256]{1,0:T(8,128)(2,1)} copy(bf16[8192,256]{0,1:T(8,128)(2,1)} %all-gather.11.cloned.1.call-done) | data formatting | bytes 8388608 | tf_op jit(solution)/shard_map/all_gather | solution.py:24
  523.7 63.6 %gather_fusion.4 = bf16[16384,256]{1,0:T(8,128)(2,1)} fusion(bf16[8192,256]{1,0:T(8,128)(2,1)} %copy.22, s32[16384]{0:T(1024)S(1)} %broadcast_clamp_fusion), kind=kCustom, calls=%fused_computation.4 | custom fusion | bytes 16842752 | tf_op jit(solution)/shard_map/gather | solution.py:16
  587.4 8.1 %fusion.13 = f32[8,256,256,1]{1,2,3,0:T(8,128)S(1)} fusion(bf16[8,8,256,256]{3,2,1,0:T(8,128)(2,1)} %param.16, bf16[8,8,256,256]{3,2,1,0:T(8,128)(2,1)} %bitcast.61), kind=kOutput, calls=%fused_computation.37 | convolution fusion | flops 2147483648 | bytes 18874368 | tf_op jit(solution)/shard_map/bnij,bnjc->bic/dot_general | solution.py:17
  595.5 0.1 fusion.7
  595.6 1.3 copy.37
  596.9 0.3 copy.39
  597.3 6.2 %add_divide_fusion = (f32[2048,128]{0,1:T(8,128)S(1)}, f32[2048,128]{0,1:T(8,128)}) fusion(f32[2048,128]{0,1:T(8,128)} %get-tuple-element.7, f32[2048,128]{0,1:T(8,128)S(1)} %copy.39, f32[2048,128]{0,1:T(8,128)} %copy.38, f32[128]{0:T(128)S(1)} %copy-done.9, f32[2048]{0:T(1024)S(1)} %copy-done.8, f32[2048,128]{0,1:T(8,128)} %get-tuple-element.19, ...), kind=kOutput, calls=%fused_computation.7 | convolution fusion | flops 541589504 | bytes 12853760 | tf_op jit(solution)/shard_map/dot_general | solution.py:32
  603.5 2.5 copy.24
  606.0 1.3 copy.25
  (38 shorter events, 0.4 us)
Async XLA Ops:
  7.2 45.3 %copy-start.1 = (f32[2048,128]{1,0:T(8,128)S(1)}, f32[2048,128]{1,0:T(8,128)}, u32[]{:S(2)}) copy-start(f32[2048,128]{1,0:T(8,128)} %param.10) | copy-start | bytes 3145732
  7.2 41.7 %copy-start = (f32[2048,128]{1,0:T(8,128)S(1)}, f32[2048,128]{1,0:T(8,128)}, u32[]{:S(2)}) copy-start(f32[2048,128]{1,0:T(8,128)} %param.11) | copy-start | bytes 3145732
  7.2 43.5 %copy-start.5 = (s32[1,8192]{1,0:T(1,128)S(1)}, s32[1,8192]{1,0:T(1,128)}, u32[]{:S(2)}) copy-start(s32[1,8192]{1,0:T(1,128)} %param.18) | copy-start | bytes 98308
  7.2 44.2 %copy-start.6 = (s32[8,8]{1,0:T(8,128)S(1)}, s32[8,8]{1,0:T(8,128)}, u32[]{:S(2)}) copy-start(s32[8,8]{1,0:T(8,128)} %param.17) | copy-start | bytes 772
  7.2 45.1 %copy-start.7 = (s32[8,8]{1,0:T(8,128)S(1)}, s32[8,8]{1,0:T(8,128)}, u32[]{:S(2)}) copy-start(s32[8,8]{1,0:T(8,128)} %param.15) | copy-start | bytes 772
  7.2 144.4 %all-gather.5.cloned.1.call-start = ((), (), s32[]{:S(2)}) async-start(), calls=%async_computation | async-start | bytes 5242880 | tf_op jit(solution)/shard_map/all_gather | solution.py:49
  11.1 215.1 %all-gather.7.cloned.1.call-start = ((), (), s32[]{:S(2)}) async-start(), calls=%async_computation.1 | async-start | bytes 5242880 | tf_op jit(solution)/shard_map/all_gather | solution.py:24
  11.1 34.2 %collective-permute-start = (bf16[2048,256]{1,0:T(8,128)(2,1)}, bf16[2048,256]{1,0:T(8,128)(2,1)S(1)}, u32[]{:S(2)}, u32[]{:S(2)}) collective-permute-start(bf16[2048,256]{1,0:T(8,128)(2,1)} %pad_maximum_fusion), channel_id=1, source_target_pairs={{0,64},{4,68},{8,72},{12,76},{16,80},{20,84},{24,88},{28,92},{32,9... | collective-permute-start | bytes 3145736 | tf_op jit(solution)/shard_map/ppermute | solution.py:11
  45.3 1.0 copy-start.3
  46.3 391.2 %all-gather.9.cloned.1.call-start = ((), (), s32[]{:S(2)}) async-start(), calls=%async_computation.2 | async-start | bytes 5242880 | tf_op jit(solution)/shard_map/all_gather | solution.py:49
  297.8 1.8 copy-start.2
  297.9 1.8 copy-start.8
  297.9 1.8 copy-start.9
  307.4 209.9 %all-gather.11.cloned.1.call-start = ((), (), s32[]{:S(2)}) async-start(), calls=%async_computation.3 | async-start | bytes 5242880 | tf_op jit(solution)/shard_map/all_gather | solution.py:24
  307.5 40.5 %collective-permute-start.1 = (bf16[2048,256]{0,1:T(8,128)(2,1)}, bf16[2048,256]{0,1:T(8,128)(2,1)S(1)}, u32[]{:S(2)}, u32[]{:S(2)}) collective-permute-start(bf16[2048,256]{0,1:T(8,128)(2,1)} %pad_maximum_fusion.1), channel_id=1, source_target_pairs={{0,64},{4,68},{8,72},{12,76},{16,80},{20,84},{24,88},{28,92},{32,9... | collective-permute-start | bytes 3145736 | tf_op jit(solution)/shard_map/ppermute | solution.py:11
  348.0 1.0 copy-start.4
Sparse Core Ops, SparseCore 0:
  11.2 52.8 all-gather.4
  65.7 38.9 all-gather.6
  307.5 51.1 all-gather.8
  360.3 35.7 all-gather.10
where the time goes:
time: 615 us; the launch traced here: 614 us
  local copies, waits for them, and re-layouts  286 us (47%)
  blocking collectives  181 us (29%)
  waiting for transfers between devices  72.3 us (12%)
  matrix products  51.7 us (8%)
  between operations  14.1 us (2%)
    gather x4, local copies, waits for them, and re-layouts, block_product(): tiles = source[indices]  254 us
    psum x2, blocking collectives, exchange_term(): weights = lax.psum(partial_sum, ('wide', 'narrow'))  181 us
    ppermute x2, waiting for transfers between devices, swapped(): lax.ppermute(array, axis, [(i, i ^ 1 << stride) for i in range(lax.axis_s...  72.2 us
    dot_general x4, matrix products, block_product(): jnp.einsum('bnij,bnjc->bic', kernel, tiles, preferred_element_type=jnp.fl...  32.4 us
    unnamed x35, local copies, waits for them, and re-layouts  17.9 us
    dot_general x2, matrix products, exchange_term(): jnp.dot(exchange_basis, weights.astype(jnp.bfloat16), preferred_element_t...  12.9 us
  transfers between devices with their start and end apart: 6, of which 2 were waited for; matrix products, arithmetic and copies ran while one was open for 27% of the time, Pallas kernels for 0%

commit v1 on v0

--- a/solution.py
+++ b/solution.py
@@ -28,7 +28,9 @@
     partial_sum = lax.dot_general(
         exchange_basis, summed, (((0,), (0,)), ((), ())), preferred_element_type=jnp.float32
     )
-    weights = lax.psum(partial_sum, ("wide", "narrow"))
+    weights = partial_sum
+    for k in ("wide", "narrow"):
+        weights = lax.psum(weights, k)
     return jnp.dot(exchange_basis, weights.astype(jnp.bfloat16), preferred_element_type=jnp.float32)
 
 

time: 615 us -> 1010 us (1.64)
  waiting for transfers between devices: 72.3 us -> 570 us
  blocking collectives: 181 us -> 82.2 us
    psum x0 -> x2, waiting for transfers between devices: none -> 504 us  [exchange_term(): weights = lax.psum(weights, k)]
    psum x2, blocking collectives: 181 us -> 82.2 us  [exchange_term(): weights = lax.psum(weights, k)]
  transfers between devices with their start and end apart: 6 -> 8, of which waited for: 2 -> 4; matrix products, arithmetic and copies ran while one was open for 27% -> 16% of each run, Pallas kernels for 0% -> 0%
where the time goes in v1:
time: 1010 us
  waiting for transfers between devices  570 us (56%)
  local copies, waits for them, and re-layouts  285 us (28%)
  blocking collectives  82.2 us (8%)
  matrix products  50.1 us (5%)
  between operations  16.1 us (2%)
    psum x2, waiting for transfers between devices, exchange_term(): weights = lax.psum(weights, k)  504 us
    gather x4, local copies, waits for them, and re-layouts, block_product(): tiles = source[indices]  254 us
    psum x2, blocking collectives, exchange_term(): weights = lax.psum(weights, k)  82.2 us
    ppermute x2, waiting for transfers between devices, swapped(): lax.ppermute(array, axis, [(i, i ^ 1 << stride) for i in range(lax.axis_s...  66.5 us
    dot_general x4, matrix products, block_product(): jnp.einsum('bnij,bnjc->bic', kernel, tiles, preferred_element_type=jnp.fl...  32.4 us
  transfers between devices with their start and end apart: 8, of which 4 were waited for; matrix products, arithmetic and copies ran while one was open for 16% of the time, Pallas kernels for 0%

profile of v1, /device:TPU:1, one launch (start us, length us, event | category | flops | bytes accessed | tf_op | source)
XLA Modules:
  0.0 1010.6 jit_solution(12026246613577305970)
XLA Ops:
  8.1 4.5 convolution_bitcast_fusion.3
  12.7 1.3 convert_element_type.24
  14.0 1.1 pad_maximum_fusion
  15.2 2.2 collective-permute-start
  17.4 32.0 %collective-permute-done = bf16[2048,256]{1,0:T(8,128)(2,1)S(1)} collective-permute-done((bf16[2048,256]{1,0:T(8,128)(2,1)}, bf16[2048,256]{1,0:T(8,128)(2,1)S(1)}, u32[]{:S(2)}, u32[]{:S(2)}) %collective-permute-start) | collective-permute-done | bytes 1048608 | tf_op jit(solution)/shard_map/ppermute | solution.py:11
  49.3 1.0 copy-done.3
  50.4 0.3 copy.12
  50.8 1.3 copy.16
  52.1 0.5 broadcast.86
  52.6 0.7 reduce.3
  53.5 0.7 gather_fusion.1
  54.4 250.8 %all-reduce.5.cloned.1.call-done = f32[1024,128]{0,1:T(8,128)} async-done(((f32[1024,128]{0,1:T(8,128)}), f32[1024,128]{0,1:T(8,128)}) %all-reduce.5.cloned.1.call-update) | async-done | bytes 524304 | tf_op jit(solution)/shard_map/psum | solution.py:33
  305.2 41.1 %all-reduce.8 = bf16[1024,128]{0,1:T(8,128)(2,1)S(1)} all-reduce(f32[1024,128]{0,1:T(8,128)} %all-reduce.5.cloned.1.call-done), channel_id=1, replica_groups=mesh['wide'=32,'narrow'=4] {'narrow'}, use_global_device_ids=true, to_apply=%region_1.0 | all-reduce | flops 131072 | bytes 786432 | tf_op jit(solution)/shard_map/psum | solution.py:33
  346.3 63.5 %gather_fusion = bf16[16384,256]{1,0:T(8,128)(2,1)} fusion(bf16[8192,256]{1,0:T(8,128)(2,1)} %all-gather.5.cloned.1.call-done, s32[16384]{0:T(1024)S(1)} %broadcast_clamp_fusion.1), kind=kCustom, calls=%fused_computation | custom fusion | bytes 16842752 | tf_op jit(solution)/shard_map/gather | solution.py:16
  409.8 8.1 fusion.10
  417.9 0.1 fusion.8
  418.1 1.4 copy.32
  419.5 1.3 copy.34
  420.8 63.5 %gather_fusion.2 = bf16[16384,256]{1,0:T(8,128)(2,1)} fusion(bf16[8192,256]{1,0:T(8,128)(2,1)} %all-gather.7.cloned.1.call-done, s32[16384]{0:T(1024)S(1)} %broadcast_clamp_fusion), kind=kCustom, calls=%fused_computation.2 | custom fusion | bytes 16842752 | tf_op jit(solution)/shard_map/gather | solution.py:16
  484.3 8.1 fusion.11
  492.4 0.1 fusion.9
  492.6 1.3 copy.33
  493.9 0.3 copy.35
  494.3 5.5 fusion.5
  499.8 1.0 copy-done.5
  500.7 0.4 copy-done.6
  501.1 1.5 convolution_bitcast_fusion.2
  502.7 1.0 pad_maximum_fusion.1
  503.8 0.3 collective-permute-start.1
  504.1 34.5 %collective-permute-done.1 = bf16[2048,256]{0,1:T(8,128)(2,1)S(1)} collective-permute-done((bf16[2048,256]{0,1:T(8,128)(2,1)}, bf16[2048,256]{0,1:T(8,128)(2,1)S(1)}, u32[]{:S(2)}, u32[]{:S(2)}) %collective-permute-start.1) | collective-permute-done | bytes 1048608 | tf_op jit(solution)/shard_map/ppermute | solution.py:11
  538.6 1.0 copy-done.4
  539.5 252.7 %all-reduce.7.cloned.1.call-done = f32[1024,128]{0,1:T(8,128)} async-done(((f32[1024,128]{0,1:T(8,128)}), f32[1024,128]{0,1:T(8,128)}) %all-reduce.7.cloned.1.call-update) | async-done | bytes 524304 | tf_op jit(solution)/shard_map/psum | solution.py:33
  792.2 41.1 %all-reduce.9 = bf16[1024,128]{0,1:T(8,128)(2,1)S(1)} all-reduce(f32[1024,128]{0,1:T(8,128)} %all-reduce.7.cloned.1.call-done), channel_id=1, replica_groups=mesh['wide'=32,'narrow'=4] {'narrow'}, use_global_device_ids=true, to_apply=%region_3.0 | all-reduce | flops 131072 | bytes 786432 | tf_op jit(solution)/shard_map/psum | solution.py:33
  833.4 6.4 copy.20
  839.7 63.5 %gather_fusion.3 = bf16[16384,256]{1,0:T(8,128)(2,1)} fusion(bf16[8192,256]{1,0:T(8,128)(2,1)} %copy.20, s32[16384]{0:T(1024)S(1)} %broadcast_clamp_fusion.1), kind=kCustom, calls=%fused_computation.3 | custom fusion | bytes 16842752 | tf_op jit(solution)/shard_map/gather | solution.py:16
  903.3 8.1 fusion.12
  911.4 0.1 fusion.6
  911.5 0.3 copy.36
  911.8 1.3 copy.38
  913.1 6.4 copy.22
  919.5 63.5 %gather_fusion.4 = bf16[16384,256]{1,0:T(8,128)(2,1)} fusion(bf16[8192,256]{1,0:T(8,128)(2,1)} %copy.22, s32[16384]{0:T(1024)S(1)} %broadcast_clamp_fusion), kind=kCustom, calls=%fused_computation.4 | custom fusion | bytes 16842752 | tf_op jit(solution)/shard_map/gather | solution.py:16
  983.0 8.1 fusion.13
  991.1 0.1 fusion.7
  991.3 1.3 copy.37
  992.6 0.3 copy.39
  993.0 6.2 add_divide_fusion
  999.2 2.5 copy.24
  1001.7 1.3 copy.25
  (48 shorter events, 0.8 us)
Async XLA Ops:
  8.0 42.4 %copy-start.1 = (f32[2048,128]{1,0:T(8,128)S(1)}, f32[2048,128]{1,0:T(8,128)}, u32[]{:S(2)}) copy-start(f32[2048,128]{1,0:T(8,128)} %param.10) | copy-start | bytes 3145732
  8.0 5.9 copy-start.2
  8.0 44.6 %copy-start.7 = (s32[1,8192]{1,0:T(1,128)S(1)}, s32[1,8192]{1,0:T(1,128)}, u32[]{:S(2)}) copy-start(s32[1,8192]{1,0:T(1,128)} %param.18) | copy-start | bytes 98308
  8.0 45.3 %copy-start.8 = (s32[8,8]{1,0:T(8,128)S(1)}, s32[8,8]{1,0:T(8,128)}, u32[]{:S(2)}) copy-start(s32[8,8]{1,0:T(8,128)} %param.17) | copy-start | bytes 772
  8.0 46.1 %copy-start.9 = (s32[8,8]{1,0:T(8,128)S(1)}, s32[8,8]{1,0:T(8,128)}, u32[]{:S(2)}) copy-start(s32[8,8]{1,0:T(8,128)} %param.15) | copy-start | bytes 772
  8.0 297.1 %all-reduce.5.cloned.1.call-start = ((), (), s32[]{:S(2)}) async-start(), calls=%async_computation.2 | async-start | bytes 1048576 | tf_op jit(solution)/shard_map/psum | solution.py:33
  12.6 333.7 %all-gather.5.cloned.1.call-start = ((), (), s32[]{:S(2)}) async-start(), calls=%async_computation | async-start | bytes 5242880 | tf_op jit(solution)/shard_map/all_gather | solution.py:51
  15.1 405.6 %all-gather.7.cloned.1.call-start = ((), (), s32[]{:S(2)}) async-start(), calls=%async_computation.1 | async-start | bytes 5242880 | tf_op jit(solution)/shard_map/all_gather | solution.py:24
  15.2 34.2 %collective-permute-start = (bf16[2048,256]{1,0:T(8,128)(2,1)}, bf16[2048,256]{1,0:T(8,128)(2,1)S(1)}, u32[]{:S(2)}, u32[]{:S(2)}) collective-permute-start(bf16[2048,256]{1,0:T(8,128)(2,1)} %pad_maximum_fusion), channel_id=1, source_target_pairs={{0,64},{4,68},{8,72},{12,76},{16,80},{20,84},{24,88},{28,92},{32,9... | collective-permute-start | bytes 3145736 | tf_op jit(solution)/shard_map/ppermute | solution.py:11
  49.3 1.0 copy-start.3
  50.4 741.9 %all-reduce.7.cloned.1.call-start = ((), (), s32[]{:S(2)}) async-start(), calls=%async_computation.5 | async-start | bytes 1048576 | tf_op jit(solution)/shard_map/psum | solution.py:33
  492.4 1.8 copy-start.10
  492.4 1.8 copy-start.11
  494.3 6.8 copy-start
  499.7 1.0 copy-start.5
  499.7 1.3 copy-start.6
  502.6 330.7 %all-gather.9.cloned.1.call-start = ((), (), s32[]{:S(2)}) async-start(), calls=%async_computation.3 | async-start | bytes 5242880 | tf_op jit(solution)/shard_map/all_gather | solution.py:51
  503.7 409.4 %all-gather.11.cloned.1.call-start = ((), (), s32[]{:S(2)}) async-start(), calls=%async_computation.4 | async-start | bytes 5242880 | tf_op jit(solution)/shard_map/all_gather | solution.py:24
  503.8 34.8 %collective-permute-start.1 = (bf16[2048,256]{0,1:T(8,128)(2,1)}, bf16[2048,256]{0,1:T(8,128)(2,1)S(1)}, u32[]{:S(2)}, u32[]{:S(2)}) collective-permute-start(bf16[2048,256]{0,1:T(8,128)(2,1)} %pad_maximum_fusion.1), channel_id=1, source_target_pairs={{0,64},{4,68},{8,72},{12,76},{16,80},{20,84},{24,88},{28,92},{32,9... | collective-permute-start | bytes 3145736 | tf_op jit(solution)/shard_map/ppermute | solution.py:11
  538.5 1.0 copy-start.4
Sparse Core Ops, SparseCore 0:
  12.7 292.3 all-reduce.4
  502.7 289.4 all-reduce.6
Sparse Core Ops, SparseCore 1:
  15.3 52.7 all-gather.4
  69.6 38.2 all-gather.6
  505.3 47.4 all-gather.8
  554.5 39.4 all-gather.10
